TPU v7x, 256 devices: a whole 4x4x8 slice. The times are simulated.
256 devices in a mesh: shift: 8 (over y_lo, x), sub: 32 (over y_hi, z, core).
Axes of the slice: x: 4, y: 4 (y_hi: 2, y_lo: 2; y = y_hi * 2 + y_lo), z: 8, core: 2. Of those that a mesh axis runs over, the one named last changes fastest.
Arguments:
- interior_rhs: bfloat16 [32, 1024, 384], P('sub'), may hold values from -6 to 6
- interface_rhs: bfloat16 [2048, 384], replicated, may hold values from -6 to 6
- interior_inverse: bfloat16 [16, 32, 1024, 1024], P('shift', 'sub'), may hold values from -0.1875 to 0.1875
- coupling: bfloat16 [32, 1024, 256], P('sub'), may hold values from -0.1875 to 0.1875
- schur_inverse: bfloat16 [16, 2048, 2048], P('shift', 'sub'), may hold values from -0.125 to 0.125
- weights: float32 [16], P('shift'), may hold values from -1 to 1
- owner_sub: int32 [32], replicated, may hold values from 0 to 31, each once
- index_blocks: int32 [32, 256], replicated, may hold values from 0 to 2047, as said below
Outputs:
- filtered: float32 [1024, 32, 384], P('shift', 'sub')
Inputs may be any that keep to these rules, and one draw needn't show every extreme that they name: `index_blocks`: each row holds 256 distinct interface unknowns; of each aligned block of 2048 // 32 interface unknowns a row holds at most 16, and exactly 16 of some block. `owner_sub`: each position names a different substructure.
All inputs are finite; a program needn't handle non-finite values.
Results may differ from a plain program's by a relative error of at most 0.0053.
Values may be sent and summed in bfloat16 or wider, within the bound.
No kernel may reach another device: no remote copies, remote signals or barrier semaphores. Data moves between devices by JAX's collectives and lax.ppermute only.
A program may use at most 64 MiB of HBM per device.

v0:
```python
import jax
import jax.numpy as jnp
from jax import lax
from jax.sharding import PartitionSpec as P


def on_device(
    interior_rhs,
    interface_rhs,
    interior_inverse,
    coupling,
    schur_inverse,
    weights,
    owner_sub,
    index_blocks,
):
    position = lax.axis_index("sub")
    substructure = lax.dynamic_index_in_dim(owner_sub, position, 0, keepdims=False)
    idx = lax.dynamic_index_in_dim(index_blocks, substructure, 0, keepdims=False)
    rhs_local = interior_rhs[0]
    couple_local = coupling[0]
    accumulated = jnp.zeros(rhs_local.shape, jnp.float32)
    for which in range(interior_inverse.shape[0]):
        inverse = interior_inverse[which, 0]
        schur_local = schur_inverse[which]
        eliminated = jnp.dot(inverse, rhs_local, preferred_element_type=jnp.float32).astype(
            jnp.bfloat16
        )
        coupled = lax.dot_general(
            couple_local, eliminated, (((0,), (0,)), ((), ())), preferred_element_type=jnp.float32
        ).astype(jnp.bfloat16)
        targets = lax.iota(jnp.int32, interface_rhs.shape[0])
        selector = (idx[None, :] == targets[:, None]).astype(jnp.bfloat16)
        summed_all = lax.psum(jnp.dot(selector, coupled, preferred_element_type=jnp.float32), "sub")
        reduced_all = (interface_rhs.astype(jnp.float32) - summed_all).astype(jnp.bfloat16)
        solved = jnp.dot(schur_local, reduced_all, preferred_element_type=jnp.float32)
        interface_sol = solved.astype(jnp.bfloat16)
        piece = lax.all_gather(interface_sol, "sub", axis=0, tiled=True)
        sources = lax.iota(jnp.int32, piece.shape[0])
        pick_selector = (idx[:, None] == sources[None, :]).astype(jnp.bfloat16)
        picked = jnp.dot(pick_selector, piece, preferred_element_type=jnp.float32)
        correction = jnp.dot(
            couple_local, picked.astype(jnp.bfloat16), preferred_element_type=jnp.float32
        ).astype(jnp.bfloat16)
        interior_sol = eliminated.astype(jnp.float32) - jnp.dot(
            inverse, correction, preferred_element_type=jnp.float32
        )
        accumulated = accumulated + weights[which] * interior_sol
    share_rows = accumulated.shape[0] // lax.axis_size("shift")
    whole_sum = lax.psum(accumulated, "shift")
    own_rows = lax.dynamic_slice_in_dim(
        whole_sum, lax.axis_index("shift") * share_rows, share_rows, 0
    )
    return own_rows[:, None, :]


def solution(mesh):
    in_specs = (
        P("sub", None, None),
        P(),
        P("shift", "sub", None, None),
        P("sub", None, None),
        P("shift", "sub", None),
        P("shift"),
        P(),
        P(),
    )
    out_specs = P("shift", "sub", None)
    return jax.shard_map(
        on_device, mesh=mesh, in_specs=in_specs, out_specs=out_specs, check_vma=False
    )
```

profile of v0, /device:TPU:32, one launch (start us, length us, event | category | flops | bytes accessed | tf_op | source)
XLA Modules:
  0.0 565.3 jit_solution(16608008642296047814)
XLA Ops:
  6.5 0.0 copy-start
  6.5 0.0 all-reduce.6.cloned.1.call-start
  6.5 1.3 dynamic_slice.11
  9.1 0.0 copy-done
  9.2 0.0 copy-start.9
  9.2 3.0 fusion.27
  12.2 0.0 copy-done.9
  12.2 0.0 copy-start.3
  12.2 0.0 copy-start.2
  12.2 1.3 fusion.30
  13.5 0.0 copy-start.5
  14.1 0.7 constant_dynamic-slice_fusion.1
  14.8 0.0 copy-done.3
  14.8 0.0 copy-done.2
  14.8 3.1 fusion.11
  17.9 0.0 copy-done.5
  17.9 3.1 fusion.10
  21.0 0.0 copy-start.1
  21.0 0.0 copy-start.7
  21.0 0.0 all-reduce.6.cloned.1.call-update
  21.0 0.0 all-gather.5.cloned.1.call-start
  21.1 283.2 %all-reduce.6.cloned.1.call-done = (f32[2048,384]{1,0:T(8,128)}, f32[2048,384]{1,0:T(8,128)}) async-done(((f32[2048,384]{1,0:T(8,128)}, f32[2048,384]{1,0:T(8,128)}), (f32[2048,384]{1,0:T(8,128)}, f32[2048,384]{1,0:T(8,128)})) %all-reduce.6.cloned.1.call-update) | async-done | bytes 6291472 | tf_op jit(solution)/shard_map/psum | solution.py:34
  304.3 0.0 copy-done.1
  304.3 0.0 copy-done.7
  304.3 3.0 fusion.41
  307.3 0.0 all-gather.5.cloned.1.call-update
  307.4 0.0 all-gather.3.cloned.1.call-start
  307.4 0.0 copy-start.8
  307.4 3.0 fusion.44
  310.4 0.0 all-gather.3.cloned.1.call-update
  310.5 0.0 all-reduce.4.cloned.1.call-start
  310.5 0.0 copy-done.8
  310.5 0.6 fusion.65
  311.1 78.0 %all-gather.5.cloned.1.call-done = bf16[2048,384]{1,0:T(8,128)(2,1)} async-done(((bf16[64,384]{1,0:T(8,128)(2,1)}), bf16[2048,384]{1,0:T(8,128)(2,1)}) %all-gather.5.cloned.1.call-update) | async-done | bytes 1572880 | tf_op jit(solution)/shard_map/all_gather | solution.py:38
  389.1 2.2 fusion.34
  391.3 4.2 fusion.2
  395.5 0.0 copy-start.4
  395.5 0.0 copy-start.6
  395.5 71.4 %all-gather.3.cloned.1.call-done = bf16[2048,384]{1,0:T(8,128)(2,1)} async-done(((bf16[64,384]{1,0:T(8,128)(2,1)}), bf16[2048,384]{1,0:T(8,128)(2,1)}) %all-gather.3.cloned.1.call-update) | async-done | bytes 1572880 | tf_op jit(solution)/shard_map/all_gather | solution.py:38
  466.9 2.2 fusion.33
  469.1 0.0 copy-done.4
  469.1 0.0 copy-done.6
  469.1 6.1 %fusion.23 = f32[1024,384]{1,0:T(8,128)} fusion(f32[384,1024]{0,1:T(8,128)} %fusion.2, bf16[1024,384]{1,0:T(8,128)(2,1)S(1)} %copy-done.6, bf16[1024,384]{1,0:T(8,128)(2,1)S(1)} %copy-done.4, bf16[2,1,1024,1024]{3,2,1,0:T(8,128)(2,1)} %param.10, bf16[256,384]{1,0:T(8,128)(2,1)S(1)} %fusion.33, f32[]{:T(128)} %bitcast.9, f32[]{:T(128)} %bitcast, ...), kind=kOutput, calls=%fused_computation.26 | convolution fusion | flops 1009778688 | bytes 7537664 | tf_op jit(solution)/shard_map/dot_general | solution.py:45
  475.2 0.0 all-reduce.4.cloned.1.call-update
  475.2 81.8 %all-reduce.4.cloned.1.call-done = f32[1024,384]{1,0:T(8,128)} async-done(((f32[1024,384]{1,0:T(8,128)}), f32[1024,384]{1,0:T(8,128)}) %all-reduce.4.cloned.1.call-update) | async-done | bytes 1572880 | tf_op jit(solution)/shard_map/psum | solution.py:50
  557.0 0.9 constant_dynamic-slice_fusion
  557.9 0.8 broadcast_in_dim.2
Async XLA Ops:
  6.5 2.6 copy-start
  6.5 297.8 %all-reduce.6.cloned.1.call-start = ((), (), s32[]{:S(2)}) async-start(), calls=%async_computation.3 | async-start | bytes 12582912 | tf_op jit(solution)/shard_map/psum | solution.py:34
  9.2 3.0 copy-start.9
  12.2 2.6 copy-start.3
  12.2 2.6 copy-start.2
  13.5 4.4 copy-start.5
  21.0 283.3 %copy-start.1 = (bf16[2048,384]{1,0:T(8,128)(2,1)S(1)}, bf16[2048,384]{1,0:T(8,128)(2,1)}, u32[]{:S(2)}) copy-start(bf16[2048,384]{1,0:T(8,128)(2,1)} %param.9) | copy-start | bytes 4718596
  21.0 283.3 %copy-start.7 = (bf16[2,64,2048]{2,1,0:T(8,128)(2,1)S(1)}, bf16[2,64,2048]{2,1,0:T(8,128)(2,1)}, u32[]{:S(2)}) copy-start(bf16[2,64,2048]{2,1,0:T(8,128)(2,1)} %param.12) | copy-start | bytes 1572868
  21.0 368.1 %all-gather.5.cloned.1.call-start = ((), (), s32[]{:S(2)}) async-start(), calls=%async_computation.1 | async-start | bytes 1622016 | tf_op jit(solution)/shard_map/all_gather | solution.py:38
  307.4 159.6 %all-gather.3.cloned.1.call-start = ((), (), s32[]{:S(2)}) async-start(), calls=%async_computation | async-start | bytes 1622016 | tf_op jit(solution)/shard_map/all_gather | solution.py:38
  307.4 3.1 copy-start.8
  310.5 246.6 %all-reduce.4.cloned.1.call-start = ((), (), s32[]{:S(2)}) async-start(), calls=%async_computation.2 | async-start | bytes 3145728 | tf_op jit(solution)/shard_map/psum | solution.py:50
  395.5 73.6 %copy-start.4 = (bf16[1024,384]{1,0:T(8,128)(2,1)S(1)}, bf16[1024,384]{1,0:T(8,128)(2,1)}, u32[]{:S(2)}) copy-start(bf16[1024,384]{1,0:T(8,128)(2,1)} %copy-done.3) | copy-start | bytes 2359300
  395.5 73.6 %copy-start.6 = (bf16[1024,384]{1,0:T(8,128)(2,1)S(1)}, bf16[1024,384]{1,0:T(8,128)(2,1)}, u32[]{:S(2)}) copy-start(bf16[1024,384]{1,0:T(8,128)(2,1)} %copy-done.5) | copy-start | bytes 2359300
Sparse Core Ops, SparseCore 0:
  21.1 283.1 all-reduce.5
  307.5 81.5 all-gather.4
  391.9 75.0 all-gather.2
  475.3 81.6 all-reduce.3
where the time goes:
time: 566 us; the launch traced here: 565 us
  waiting for transfers between devices  515 us (91%)
  matrix products  31 us (5%)
  between operations  15.2 us (3%)
    psum x1, waiting for transfers between devices, on_device(): lax.psum(jnp.dot(selector, coupled, preferred_element_type=jnp.float32),...  283 us
    all_gather x2, waiting for transfers between devices, on_device(): piece = lax.all_gather(interface_sol, 'sub', axis=0, tiled=True)  149 us
    psum x1, waiting for transfers between devices, on_device(): whole_sum = lax.psum(accumulated, 'shift')  81.8 us
  transfers between devices with their start and end apart: 4, of which 4 were waited for; matrix products, arithmetic and copies ran while one was open for 2% of the time, Pallas kernels for 0%

commit v1 on v0

--- a/solution.py
+++ b/solution.py
@@ -35,7 +35,8 @@
         reduced_all = (interface_rhs.astype(jnp.float32) - summed_all).astype(jnp.bfloat16)
         solved = jnp.dot(schur_local, reduced_all, preferred_element_type=jnp.float32)
         interface_sol = solved.astype(jnp.bfloat16)
-        piece = lax.all_gather(interface_sol, "sub", axis=0, tiled=True)
+        sent = jnp.stack([interface_sol] * lax.axis_size("sub"))
+        piece = jnp.concatenate(lax.all_to_all(sent, "sub", 0, 0), axis=0)
         sources = lax.iota(jnp.int32, piece.shape[0])
         pick_selector = (idx[:, None] == sources[None, :]).astype(jnp.bfloat16)
         picked = jnp.dot(pick_selector, piece, preferred_element_type=jnp.float32)

time: 566 us -> 505 us (0.89)
  waiting for transfers between devices: 515 us -> 437 us
  starting transfers between devices: 0.13 us -> 16.4 us
    all_gather x2 -> x0, waiting for transfers between devices: 149 us -> none  [on_device(): piece = lax.all_gather(interface_sol, 'sub', axis=0, tiled=True)]
    all_to_all x0 -> x2, waiting for transfers between devices: none -> 73.8 us  [on_device(): piece = jnp.concatenate(lax.all_to_all(sent, 'sub', 0, 0), axis=0)]
    all_to_all x0 -> x2, starting transfers between devices: none -> 16.3 us  [on_device(): piece = jnp.concatenate(lax.all_to_all(sent, 'sub', 0, 0), axis=0)]
where the time goes in v1:
time: 505 us; the launch traced here: 504 us
  waiting for transfers between devices  437 us (87%)
  matrix products  28.5 us (6%)
  starting transfers between devices  16.4 us (3%)
  between operations  15.5 us (3%)
  local copies, waits for them, and re-layouts  7.22 us (1%)
    psum x1, waiting for transfers between devices, on_device(): lax.psum(jnp.dot(selector, coupled, preferred_element_type=jnp.float32),...  283 us
    psum x1, waiting for transfers between devices, on_device(): whole_sum = lax.psum(accumulated, 'shift')  79.4 us
    all_to_all x2, waiting for transfers between devices, on_device(): piece = jnp.concatenate(lax.all_to_all(sent, 'sub', 0, 0), axis=0)  73.8 us
    all_to_all x2, starting transfers between devices, on_device(): piece = jnp.concatenate(lax.all_to_all(sent, 'sub', 0, 0), axis=0)  16.3 us
    dot_general x2, matrix products, on_device(): jnp.dot(inverse, correction, preferred_element_type=jnp.float32)  10.7 us
  transfers between devices with their start and end apart: 4, of which 4 were waited for; matrix products, arithmetic and copies ran while one was open for 2% of the time, Pallas kernels for 0%

profile of v1, /device:TPU:32, one launch (start us, length us, event | category | flops | bytes accessed | tf_op | source)
XLA Modules:
  0.0 504.2 jit_solution(2190951365067894674)
XLA Ops:
  6.5 0.0 copy-start
  6.5 0.0 all-reduce.6.cloned.1.call-start
  6.5 1.3 dynamic_slice.11
  9.1 0.0 copy-done
  9.2 0.0 copy-start.7
  9.2 3.0 fusion.27
  12.2 0.0 copy-done.7
  12.2 0.0 copy-start.3
  12.2 0.0 copy-start.2
  12.2 1.3 fusion.30
  13.5 0.0 copy-start.4
  14.1 0.7 constant_dynamic-slice_fusion.1
  14.8 0.0 copy-done.3
  14.8 0.0 copy-done.2
  14.8 3.0 fusion.11
  17.9 0.0 copy-done.4
  17.9 3.1 fusion.10
  21.0 0.0 copy-start.1
  21.0 0.0 copy-start.5
  21.0 0.0 all-reduce.6.cloned.1.call-update
  21.0 283.3 %all-reduce.6.cloned.1.call-done = (f32[2048,384]{1,0:T(8,128)}, f32[2048,384]{1,0:T(8,128)}) async-done(((f32[2048,384]{1,0:T(8,128)}, f32[2048,384]{1,0:T(8,128)}), (f32[2048,384]{1,0:T(8,128)}, f32[2048,384]{1,0:T(8,128)})) %all-reduce.6.cloned.1.call-update) | async-done | bytes 6291472 | tf_op jit(solution)/shard_map/psum | solution.py:34
  304.3 0.0 copy-done.1
  304.3 0.0 copy-done.5
  304.3 2.3 fusion.41
  306.6 1.4 stack.5
  308.0 12.6 %all-to-all-start.1 = ((bf16[32,64,384]{2,1,0:T(8,128)(2,1)}), bf16[32,64,384]{2,1,0:T(8,128)(2,1)}, u32[]{:S(2)}, u32[]{:S(2)}) async-start(bf16[32,64,384]{2,1,0:T(8,128)(2,1)} %stack.5), calls=%async_computation.1 | async-start | bytes 3145728 | tf_op jit(solution)/shard_map/all_to_all | solution.py:39
  320.6 2.3 fusion.44
  322.9 0.0 copy-start.6
  322.9 39.4 %all-to-all-done.1 = bf16[32,64,384]{2,1,0:T(8,128)(2,1)} async-done(((bf16[32,64,384]{2,1,0:T(8,128)(2,1)}), bf16[32,64,384]{2,1,0:T(8,128)(2,1)}, u32[]{:S(2)}, u32[]{:S(2)}) %all-to-all-start.1) | async-done | bytes 1572896 | tf_op jit(solution)/shard_map/all_to_all | solution.py:39
  362.4 1.4 stack.4
  363.8 3.8 all-to-all-start
  367.5 0.0 all-reduce.4.cloned.1.call-start
  367.6 0.0 copy-done.6
  367.6 0.6 fusion.65
  368.2 2.2 fusion.34
  370.4 4.2 fusion.2
  374.6 34.4 %all-to-all-done = bf16[32,64,384]{2,1,0:T(8,128)(2,1)S(1)} async-done(((bf16[32,64,384]{2,1,0:T(8,128)(2,1)}), bf16[32,64,384]{2,1,0:T(8,128)(2,1)S(1)}, u32[]{:S(2)}, u32[]{:S(2)}) %all-to-all-start) | async-done | bytes 1572896 | tf_op jit(solution)/shard_map/all_to_all | solution.py:39
  408.9 0.8 fusion.33
  409.7 6.4 %fusion.23 = f32[1024,384]{1,0:T(8,128)} fusion(f32[384,1024]{0,1:T(8,128)} %fusion.2, bf16[1024,384]{1,0:T(8,128)(2,1)} %copy-done.4, bf16[1024,384]{1,0:T(8,128)(2,1)} %copy-done.3, bf16[2,1,1024,1024]{3,2,1,0:T(8,128)(2,1)} %param.10, bf16[256,384]{1,0:T(8,128)(2,1)S(1)} %fusion.33, f32[]{:T(128)} %bitcast.10, f32[]{:T(128)} %bitcast, ...), kind=kOutput, calls=%fused_computation.26 | convolution fusion | flops 1009778688 | bytes 7537664 | tf_op jit(solution)/shard_map/dot_general | solution.py:46
  416.1 0.0 all-reduce.4.cloned.1.call-update
  416.2 79.4 %all-reduce.4.cloned.1.call-done = f32[1024,384]{1,0:T(8,128)} async-done(((f32[1024,384]{1,0:T(8,128)}), f32[1024,384]{1,0:T(8,128)}) %all-reduce.4.cloned.1.call-update) | async-done | bytes 1572880 | tf_op jit(solution)/shard_map/psum | solution.py:51
  495.6 0.9 constant_dynamic-slice_fusion
  496.5 0.8 broadcast_in_dim.2
Async XLA Ops:
  6.5 2.6 copy-start
  6.5 297.7 %all-reduce.6.cloned.1.call-start = ((), (), s32[]{:S(2)}) async-start(), calls=%async_computation.3 | async-start | bytes 12582912 | tf_op jit(solution)/shard_map/psum | solution.py:34
  9.2 3.0 copy-start.7
  12.2 2.6 copy-start.3
  12.2 2.6 copy-start.2
  13.5 4.4 copy-start.4
  21.0 283.3 %copy-start.1 = (bf16[2048,384]{1,0:T(8,128)(2,1)S(1)}, bf16[2048,384]{1,0:T(8,128)(2,1)}, u32[]{:S(2)}) copy-start(bf16[2048,384]{1,0:T(8,128)(2,1)} %param.9) | copy-start | bytes 4718596
  21.0 283.3 %copy-start.5 = (bf16[2,64,2048]{2,1,0:T(8,128)(2,1)S(1)}, bf16[2,64,2048]{2,1,0:T(8,128)(2,1)}, u32[]{:S(2)}) copy-start(bf16[2,64,2048]{2,1,0:T(8,128)(2,1)} %param.12) | copy-start | bytes 1572868
  308.0 54.4 %all-to-all-start.1 = ((bf16[32,64,384]{2,1,0:T(8,128)(2,1)}), bf16[32,64,384]{2,1,0:T(8,128)(2,1)}, u32[]{:S(2)}, u32[]{:S(2)}) async-start(bf16[32,64,384]{2,1,0:T(8,128)(2,1)} %stack.5), calls=%async_computation.1 | async-start | bytes 3145728 | tf_op jit(solution)/shard_map/all_to_all | solution.py:39
  322.9 44.7 %copy-start.6 = (f32[2]{0:T(128)S(1)}, f32[2]{0:T(128)}, u32[]{:S(2)}) copy-start(f32[2]{0:T(128)} %param.13) | copy-start | bytes 28
  363.8 45.2 %all-to-all-start = ((bf16[32,64,384]{2,1,0:T(8,128)(2,1)}), bf16[32,64,384]{2,1,0:T(8,128)(2,1)S(1)}, u32[]{:S(2)}, u32[]{:S(2)}) async-start(bf16[32,64,384]{2,1,0:T(8,128)(2,1)} %stack.4), calls=%async_computation | async-start | bytes 3145728 | tf_op jit(solution)/shard_map/all_to_all | solution.py:39
  367.5 128.0 %all-reduce.4.cloned.1.call-start = ((), (), s32[]{:S(2)}) async-start(), calls=%async_computation.2 | async-start | bytes 3145728 | tf_op jit(solution)/shard_map/psum | solution.py:51
Sparse Core Ops, SparseCore 0:
  21.1 283.1 all-reduce.5
  416.3 79.2 all-reduce.3
